TPU v7x, 32 devices: a whole 2x2x4 slice. The times are simulated.
32 devices in a mesh: groups: 1, wide: 16 (over z, y, core), tp: 2 (over x), sub: 1.
Axes of the slice: x: 2, y: 2, z: 4, core: 2. Of those that a mesh axis runs over, the one named last changes fastest.
Arguments:
- moe_input: bfloat16 [128, 3584], P(('groups', 'wide', 'tp', 'sub')), may hold values from -6 to 6
- routes: int32 [128, 8], P(('groups', 'wide', 'tp', 'sub')), may hold values from 0 to 15, all different within a row; in each aligned block of 4 rows (0 to 3, 4 to 7, ...) at most 4 rows name the same one
- router_weight: bfloat16 [3584, 16], replicated, may hold values from -0.1875 to 0.1875
- gate_weight: bfloat16 [16, 3584, 1024], P('wide', None, ('tp', 'sub')), may hold values from -0.09375 to 0.09375
- up_weight: bfloat16 [16, 3584, 1024], P('wide', None, ('tp', 'sub')), may hold values from -0.09375 to 0.09375
- down_weight: bfloat16 [16, 1024, 3584], P('wide', ('tp', 'sub')), may hold values from -0.1875 to 0.1875
- query_latent: bfloat16 [16, 128, 512], P(('groups', 'wide', 'sub')), may hold values from -20 to 20
- query_rope: bfloat16 [16, 64, 128], P(('groups', 'wide', 'sub')), may hold values from -6 to 6
- cache_latent: bfloat16 [16, 4096, 512], P(('groups', 'wide', 'sub'), 'tp'), may hold values from -6 to 6
- cache_rope: bfloat16 [16, 64, 4096], P(('groups', 'wide', 'sub'), None, 'tp'), may hold values from -6 to 6
- cache_lengths: int32 [16], P(('groups', 'wide', 'sub')), may hold values from 256 to 4096, as said below
Outputs:
- moe_out: bfloat16 [128, 3584], P(('groups', 'wide', 'tp', 'sub'))
- att_out: bfloat16 [16, 128, 512], P(('groups', 'wide', 'sub'))
Inputs may be any that keep to these rules, and one draw needn't show every extreme that they name: `routes`: within the 4 rows of one device no expert is named by more than 4 rows, and in some device's rows an expert is named by exactly 4 of them. Row r attends to its cached positions 0 to cache_lengths[r] - 1; in every draw some row has exactly 4096.
All inputs are finite; a program needn't handle non-finite values.
Results may differ from a plain program's by a relative error of at most 0.015.
Values may be sent and summed in bfloat16 or wider, within the bound.
No kernel may reach another device: no remote copies, remote signals or barrier semaphores. Data moves between devices by JAX's collectives and lax.ppermute only.
A program may use at most 64 MiB of HBM per device.

v0:
```python
import jax
import jax.numpy as jnp
from jax import lax
from jax.sharding import PartitionSpec as P

score_scale = 0.07216878364870323
route_scale = 2.5


def slot_tables(route_block, experts, capacity):
    entries, picks = route_block.shape
    flattened = route_block.reshape(entries * picks)
    expert_ids = jnp.arange(experts, dtype=jnp.int32)
    onehot = (flattened[:, None] == expert_ids[None, :]).astype(jnp.int32)
    earlier = jnp.cumsum(onehot, axis=0) - onehot
    position = jnp.sum(earlier * onehot, axis=1)
    target = flattened * capacity + position
    slot_ids = jnp.arange(experts * capacity, dtype=jnp.int32)
    select = (target[:, None] == slot_ids[None, :]).astype(jnp.float32)
    return (
        select.reshape(entries, picks, experts * capacity),
        onehot.reshape(entries, picks, experts).astype(jnp.float32),
    )


def expert_part(row_block, gate_slice, up_slice, down_slice):
    gate_value = jnp.dot(row_block, gate_slice, preferred_element_type=jnp.float32)
    up_value = jnp.dot(row_block, up_slice, preferred_element_type=jnp.float32)
    hidden = (jax.nn.silu(gate_value) * up_value).astype(jnp.bfloat16)
    return jnp.dot(hidden, down_slice, preferred_element_type=jnp.float32).astype(jnp.bfloat16)


def body(
    moe_input,
    routes,
    router_weight,
    gate_weight,
    up_weight,
    down_weight,
    query_latent,
    query_rope,
    cache_latent,
    cache_rope,
    cache_lengths,
):
    experts = lax.axis_size("wide") * gate_weight.shape[0]
    row_count, picks = routes.shape
    width = moe_input.shape[1]
    capacity = min(row_count, max(2, 2 * row_count * picks // experts))
    select, picked = slot_tables(routes, experts, capacity)
    logits = jnp.dot(moe_input, router_weight, preferred_element_type=jnp.float32)
    probs = jax.nn.sigmoid(logits)
    chosen = jnp.sum(picked * probs[:, None, :], axis=2)
    gates = route_scale * chosen / jnp.sum(chosen, axis=1, keepdims=True)
    spread_rows = jnp.sum(select, axis=1).T.astype(jnp.bfloat16)
    weighting = jnp.sum(gates[:, :, None] * select, axis=1)
    gate_slice = gate_weight[0]
    up_slice = up_weight[0]
    down_slice = down_weight[0]
    packed = jnp.dot(spread_rows, moe_input, preferred_element_type=jnp.float32)
    packed = packed.astype(jnp.bfloat16).reshape(experts, capacity, width)
    arrived = lax.all_to_all(packed, "wide", split_axis=0, concat_axis=0, tiled=True)
    column = lax.all_gather(arrived, ("tp", "sub"), axis=0, tiled=True)
    flattened = column.reshape(-1, width)
    summed = lax.psum_scatter(
        expert_part(flattened, gate_slice, up_slice, down_slice)
        .astype(jnp.float32)
        .astype(jnp.bfloat16),
        ("tp", "sub"),
        scatter_dimension=0,
        tiled=True,
    )
    own_out = summed.reshape(arrived.shape[0], capacity, width)
    returned = lax.all_to_all(own_out, "wide", split_axis=0, concat_axis=0, tiled=True)
    outputs = returned.reshape(experts * capacity, width)
    combined = jnp.dot(weighting, outputs.astype(jnp.float32), precision=lax.Precision.HIGHEST)
    moe_out = combined.astype(jnp.bfloat16)
    local_len = cache_latent.shape[1]
    positions = lax.axis_index("tp") * local_len + jnp.arange(local_len, dtype=jnp.int32)
    scores = jnp.einsum(
        "rhc,rlc->rhl", query_latent, cache_latent, preferred_element_type=jnp.float32
    )
    scores = (
        scores
        + jnp.einsum("rkh,rkl->rhl", query_rope, cache_rope, preferred_element_type=jnp.float32)
    ) * score_scale
    live = positions[None, None, :] < cache_lengths[:, None, None]
    masked = jnp.where(live, scores, -1e30)
    peak = lax.pmax(jnp.max(masked, axis=2), "tp")
    weights = jnp.where(live, jnp.exp(masked - peak[:, :, None]), 0.0)
    denom = jnp.sum(weights, axis=2)
    mixed = jnp.einsum(
        "rhl,rlc->rhc",
        weights.astype(jnp.bfloat16),
        cache_latent,
        preferred_element_type=jnp.float32,
    )
    mixed, denom = (
        lax.psum(mixed.astype(jnp.bfloat16), "tp").astype(jnp.float32),
        lax.psum(denom.astype(jnp.bfloat16), "tp").astype(jnp.float32),
    )
    att_out = (mixed / denom[:, :, None]).astype(jnp.bfloat16)
    return (moe_out, att_out)


def solution(mesh):
    in_specs = (
        P(("groups", "wide", "tp", "sub"), None),
        P(("groups", "wide", "tp", "sub"), None),
        P(),
        P("wide", None, ("tp", "sub")),
        P("wide", None, ("tp", "sub")),
        P("wide", ("tp", "sub"), None),
        P(("groups", "wide", "sub"), None, None),
        P(("groups", "wide", "sub"), None, None),
        P(("groups", "wide", "sub"), "tp", None),
        P(("groups", "wide", "sub"), None, "tp"),
        P(("groups", "wide", "sub")),
    )
    out_specs = (P(("groups", "wide", "tp", "sub"), None), P(("groups", "wide", "sub"), None, None))
    return jax.shard_map(body, mesh=mesh, in_specs=in_specs, out_specs=out_specs, check_vma=False)
```

profile of v0, /device:TPU:0, one launch (start us, length us, event | category | flops | bytes accessed | tf_op | source)
XLA Modules:
  0.0 122.5 jit_solution(11289063658092021254)
XLA Ops:
  7.2 0.0 copy-start
  7.2 0.0 reduce-scatter.2.cloned.1.call-start
  7.2 0.9 eq.36
  8.1 0.1 fusion.45
  8.2 0.1 reduce_window_sum.11
  8.3 0.2 select_reduce_fusion.1
  8.4 0.1 reduce_sum.57
  8.5 0.7 multiply_add_fusion
  9.2 1.1 fusion.25
  10.3 0.9 fusion.43
  11.2 0.1 multiply_divide_fusion
  11.2 0.1 convert_reduce_fusion
  11.3 1.1 convolution_convert_fusion.1
  12.4 0.1 reshape.119
  12.5 20.4 %all_to_all.10 = bf16[16,4,3584]{2,1,0:T(4,128)(2,1)S(1)} all-to-all(bf16[16,4,3584]{2,1,0:T(4,128)(2,1)S(1)} %reshape.119), channel_id=1, replica_groups=mesh['groups'=1,'wide'=16,'tp'=2,'sub'=1] {'wide'}, dimensions={0} | all-to-all | bytes 917504 | tf_op jit(solution)/shard_map/all_to_all | solution.py:62
  33.0 13.3 %all_gather.3 = bf16[32,4,3584]{2,1,0:T(4,128)(2,1)} all-gather(bf16[16,4,3584]{2,1,0:T(4,128)(2,1)S(1)} %all_to_all.10), channel_id=1, replica_groups=mesh['groups'=1,'wide'=16,'tp'=2,'sub'=1] {'tp','sub'}, dimensions={0}, use_global_device_ids=true | all-gather | bytes 1376256 | tf_op jit(solution)/shard_map/all_gather | solution.py:63
  46.3 1.7 %reshape.120 = bf16[128,3584]{1,0:T(8,128)(2,1)S(1)} reshape(bf16[32,4,3584]{2,1,0:T(4,128)(2,1)} %all_gather.3) | data formatting | bytes 1835008 | tf_op jit(solution)/shard_map/reshape | solution.py:64
  47.9 2.7 %fusion.3 = f32[128,512]{1,0:T(8,128)S(1)} fusion(bf16[128,3584]{1,0:T(8,128)(2,1)S(1)} %reshape.120, bf16[1,3584,512]{2,1,0:T(8,128)(2,1)} %param.14), kind=kOutput, calls=%fused_computation.6 | convolution fusion | flops 469762048 | bytes 4849664 | tf_op jit(solution)/shard_map/dot_general | solution.py:27
  50.6 0.0 copy-start.2
  50.6 5.4 %convolution_convert_fusion = bf16[128,3584]{1,0:T(8,128)(2,1)} fusion(bf16[1,512,3584]{2,1,0:T(8,128)(2,1)} %param.16, bf16[128,3584]{1,0:T(8,128)(2,1)S(1)} %reshape.120, bf16[1,3584,512]{2,1,0:T(8,128)(2,1)} %param.15, f32[128,512]{1,0:T(8,128)S(1)} %fusion.3), kind=kOutput, calls=%fused_computation | convolution fusion | flops 940376064 | bytes 9437184 | tf_op jit(solution)/shard_map/dot_general | solution.py:30
  56.0 0.0 copy-start.1
  56.0 0.0 reduce-scatter.2.cloned.1.call-update
  56.7 0.0 copy-done
  56.8 0.0 copy-done.2
  56.8 1.8 %fusion.9 = f32[128,2048]{1,0:T(8,128)} fusion(bf16[1,2048,512]{2,1,0:T(8,128)(2,1)S(1)} %copy-done, bf16[1,128,512]{2,1,0:T(8,128)(2,1)S(1)} %copy-done.2), kind=kOutput, calls=%fused_computation.13 | convolution fusion | flops 268435456 | bytes 3276800 | tf_op jit(solution)/shard_map/rhc,rlc->rhl/dot_general | solution.py:80
  58.6 16.0 %reduce-scatter.2.cloned.1.call-done = bf16[64,3584]{1,0:T(8,128)(2,1)} async-done(((bf16[128,3584]{1,0:T(8,128)(2,1)}), bf16[64,3584]{1,0:T(8,128)(2,1)}) %reduce-scatter.2.cloned.1.call-update) | async-done | bytes 458768 | tf_op jit(solution)/shard_map/reduce_scatter | solution.py:65
  74.5 1.9 %reshape.121 = bf16[16,4,3584]{2,1,0:T(4,128)(2,1)} reshape(bf16[64,3584]{1,0:T(8,128)(2,1)} %reduce-scatter.2.cloned.1.call-done) | data formatting | bytes 917504 | tf_op jit(solution)/shard_map/reshape | solution.py:73
  76.4 5.7 %all-to-all-start.1 = ((bf16[16,4,3584]{2,1,0:T(4,128)(2,1)}), bf16[16,4,3584]{2,1,0:T(4,128)(2,1)}, u32[]{:S(2)}, u32[]{:S(2)}) async-start(bf16[16,4,3584]{2,1,0:T(4,128)(2,1)} %reshape.121), calls=%async_computation.2 | async-start | bytes 917504 | tf_op jit(solution)/shard_map/all_to_all | solution.py:74
  82.1 0.0 all-reduce.2.cloned.1.call-start
  82.1 0.0 copy-done.1
  82.2 1.7 %fusion.49 = (f32[128]{0:T(128)S(1)}, f32[128,2048]{1,0:T(8,128)S(1)}) fusion(f32[128,2048]{1,0:T(8,128)} %fusion.9, bf16[1,64,2048]{2,1,0:T(8,128)(2,1)S(1)} %copy-done.1, bf16[1,64,128]{2,1,0:T(8,128)(2,1)} %param.18, pred[2048]{0:T(1024)(128)(4,1)S(1)} %add_compare_fusion), kind=kOutput, calls=%fused_computation.55 | convolution fusion | flops 34602880 | bytes 2378240 | tf_op jit(solution)/shard_map/rkh,rkl->rhl/dot_general | solution.py:85
  83.8 4.9 %pmax.7 = f32[128]{0:T(128)S(1)} all-reduce(f32[128]{0:T(128)S(1)} %get-tuple-element.6), channel_id=1, replica_groups=mesh['groups'=1,'wide'=16,'tp'=2,'sub'=1] {'tp'}, use_global_device_ids=true, to_apply=%region_8.9 | all-reduce | flops 128 | bytes 1024 | tf_op jit(solution)/shard_map/pmax | solution.py:89
  88.8 1.2 fusion.20
  89.9 0.0 all-reduce.2.cloned.1.call-update
  89.9 0.3 fusion.28
  90.3 4.9 %psum.15 = bf16[128]{0:T(256)(128)(2,1)S(1)} all-reduce(bf16[128]{0:T(256)(128)(2,1)S(1)} %fusion.28), channel_id=1, replica_groups=mesh['groups'=1,'wide'=16,'tp'=2,'sub'=1] {'tp'}, use_global_device_ids=true, to_apply=%region_11.12 | all-reduce | flops 128 | bytes 512 | tf_op jit(solution)/shard_map/psum | solution.py:100
  95.2 16.8 %all-reduce.2.cloned.1.call-done = bf16[1,128,512]{2,1,0:T(8,128)(2,1)} async-done(((bf16[1,128,512]{2,1,0:T(8,128)(2,1)}), bf16[1,128,512]{2,1,0:T(8,128)(2,1)}) %all-reduce.2.cloned.1.call-update) | async-done | bytes 131088 | tf_op jit(solution)/shard_map/psum | solution.py:99
  112.0 1.7 %divide_convert_fusion = bf16[1,128,512]{2,1,0:T(8,128)(2,1)} fusion(bf16[1,128,512]{2,1,0:T(8,128)(2,1)} %all-reduce.2.cloned.1.call-done, f32[128]{0:T(128)S(1)} %div.36), kind=kLoop, calls=%fused_computation.30 | loop fusion | flops 196608 | bytes 262656 | tf_op jit(solution)/shard_map/convert_element_type | solution.py:102
  113.6 0.0 all-to-all-done.1
  113.7 1.1 reshape.122
  114.8 0.9 convolution_convert_fusion.2
  (2 shorter events, 0.0 us)
Async XLA Ops:
  7.2 49.6 %copy-start = (bf16[1,2048,512]{2,1,0:T(8,128)(2,1)S(1)}, bf16[1,2048,512]{2,1,0:T(8,128)(2,1)}, u32[]{:S(2)}) copy-start(bf16[1,2048,512]{2,1,0:T(8,128)(2,1)} %param.19) | copy-start | bytes 6291460
  7.2 67.3 %reduce-scatter.2.cloned.1.call-start = ((), (), s32[]{:S(2)}) async-start(), calls=%async_computation.3 | async-start | bytes 1376256 | tf_op jit(solution)/shard_map/reduce_scatter | solution.py:65
  50.6 6.1 %copy-start.2 = (bf16[1,128,512]{2,1,0:T(8,128)(2,1)S(1)}, bf16[1,128,512]{2,1,0:T(8,128)(2,1)}, u32[]{:S(2)}) copy-start(bf16[1,128,512]{2,1,0:T(8,128)(2,1)} %param.17) | copy-start | bytes 393220
  56.0 26.1 %copy-start.1 = (bf16[1,64,2048]{2,1,0:T(8,128)(2,1)S(1)}, bf16[1,64,2048]{2,1,0:T(8,128)(2,1)}, u32[]{:S(2)}) copy-start(bf16[1,64,2048]{2,1,0:T(8,128)(2,1)} %param.20) | copy-start | bytes 786436
  76.4 37.2 %all-to-all-start.1 = ((bf16[16,4,3584]{2,1,0:T(4,128)(2,1)}), bf16[16,4,3584]{2,1,0:T(4,128)(2,1)}, u32[]{:S(2)}, u32[]{:S(2)}) async-start(bf16[16,4,3584]{2,1,0:T(4,128)(2,1)} %reshape.121), calls=%async_computation.2 | async-start | bytes 917504 | tf_op jit(solution)/shard_map/all_to_all | solution.py:74
  82.1 29.9 %all-reduce.2.cloned.1.call-start = ((), (), s32[]{:S(2)}) async-start(), calls=%async_computation.4 | async-start | bytes 262144 | tf_op jit(solution)/shard_map/psum | solution.py:99
Sparse Core Ops, SparseCore 0:
  56.2 18.3 reduce-scatter.1
  90.1 21.8 all-reduce.1
where the time goes:
time: 123 us
  blocking collectives  43.6 us (35%)
  waiting for transfers between devices  32.8 us (27%)
  matrix products  15.7 us (13%)
  between operations  14.8 us (12%)
  local copies, waits for them, and re-layouts  5.8 us (5%)
  starting transfers between devices  5.74 us (5%)
  other arithmetic  4.05 us (3%)
    all_to_all x1, blocking collectives, body(): lax.all_to_all(packed, 'wide', split_axis=0, concat_axis=0, tiled=True)  20.4 us
    psum x1, waiting for transfers between devices, body(): lax.psum(mixed.astype(jnp.bfloat16), 'tp').astype(jnp.float32)  16.8 us
    reduce_scatter x1, waiting for transfers between devices, body(): lax.psum_scatter(expert_part(flattened, gate_slice, up_slice, down_slice)...  16 us
    all_gather x1, blocking collectives, body(): column = lax.all_gather(arrived, ('tp', 'sub'), axis=0, tiled=True)  13.3 us
    all_to_all x1, starting transfers between devices, body(): lax.all_to_all(own_out, 'wide', split_axis=0, concat_axis=0, tiled=True)  5.66 us
    dot_general x1, matrix products, expert_part(): jnp.dot(hidden, down_slice, preferred_element_type=jnp.float32)  5.39 us
    pmax x1, blocking collectives, body(): peak = lax.pmax(jnp.max(masked, axis=2), 'tp')  4.93 us
    psum x1, blocking collectives, body(): lax.psum(denom.astype(jnp.bfloat16), 'tp').astype(jnp.float32)  4.93 us
  transfers between devices with their start and end apart: 3, of which 2 were waited for; matrix products, arithmetic and copies ran while one was open for 5% of the time, Pallas kernels for 0%

commit v1 on v0

--- a/solution.py
+++ b/solution.py
@@ -95,8 +95,12 @@
         cache_latent,
         preferred_element_type=jnp.float32,
     )
+
+    def keep_up_figure_up(z_in, mesh_ax):
+        return jnp.sum(jax.lax.all_gather(z_in, mesh_ax), 0)
+
     mixed, denom = (
-        lax.psum(mixed.astype(jnp.bfloat16), "tp").astype(jnp.float32),
+        keep_up_figure_up(mixed.astype(jnp.bfloat16), "tp").astype(jnp.float32),
         lax.psum(denom.astype(jnp.bfloat16), "tp").astype(jnp.float32),
     )
     att_out = (mixed / denom[:, :, None]).astype(jnp.bfloat16)

time: 123 us -> 110 us (0.89)
  waiting for transfers between devices: 32.8 us -> 16 us
  blocking collectives: 43.6 us -> 49.2 us
    psum x1 -> x0, waiting for transfers between devices: 16.8 us -> none  [body(): lax.psum(mixed.astype(jnp.bfloat16), 'tp').astype(jnp.float32)]
    all_gather x0 -> x1, blocking collectives: none -> 5.64 us  [keep_up_figure_up(): return jnp.sum(jax.lax.all_gather(z_in, mesh_ax), 0)]
  transfers between devices with their start and end apart: 3 -> 2, of which waited for: 2 -> 1; matrix products, arithmetic and copies ran while one was open for 5% -> 5% of each run, Pallas kernels for 0% -> 0%
where the time goes in v1:
time: 110 us
  blocking collectives  49.2 us (45%)
  waiting for transfers between devices  16 us (15%)
  matrix products  15.1 us (14%)
  between operations  14.8 us (13%)
  local copies, waits for them, and re-layouts  5.8 us (5%)
  starting transfers between devices  5.69 us (5%)
  other arithmetic  3.19 us (3%)
    all_to_all x1, blocking collectives, body(): lax.all_to_all(packed, 'wide', split_axis=0, concat_axis=0, tiled=True)  20.4 us
    reduce_scatter x1, waiting for transfers between devices, body(): lax.psum_scatter(expert_part(flattened, gate_slice, up_slice, down_slice)...  16 us
    all_gather x1, blocking collectives, body(): column = lax.all_gather(arrived, ('tp', 'sub'), axis=0, tiled=True)  13.3 us
    all_to_all x1, starting transfers between devices, body(): lax.all_to_all(own_out, 'wide', split_axis=0, concat_axis=0, tiled=True)  5.65 us
    all_gather x1, blocking collectives, keep_up_figure_up(): return jnp.sum(jax.lax.all_gather(z_in, mesh_ax), 0)  5.64 us
    dot_general x1, matrix products, expert_part(): jnp.dot(hidden, down_slice, preferred_element_type=jnp.float32)  5.4 us
    pmax x1, blocking collectives, body(): peak = lax.pmax(jnp.max(masked, axis=2), 'tp')  4.93 us
    psum x1, blocking collectives, body(): lax.psum(denom.astype(jnp.bfloat16), 'tp').astype(jnp.float32)  4.93 us
  transfers between devices with their start and end apart: 2, of which 1 were waited for; matrix products, arithmetic and copies ran while one was open for 5% of the time, Pallas kernels for 0%

profile of v1, /device:TPU:0, one launch (start us, length us, event | category | flops | bytes accessed | tf_op | source)
XLA Modules:
  0.0 109.8 jit_solution(14051981083115423527)
XLA Ops:
  7.2 0.0 copy-start
  7.2 0.0 reduce-scatter.2.cloned.1.call-start
  7.2 0.9 eq.36
  8.1 0.1 fusion.43
  8.2 0.1 reduce_window_sum.11
  8.3 0.2 select_reduce_fusion.1
  8.4 0.1 reduce_sum.69
  8.5 0.7 multiply_add_fusion
  9.2 1.1 fusion.22
  10.3 0.9 fusion.41
  11.2 0.1 multiply_divide_fusion
  11.2 0.1 convert_reduce_fusion
  11.3 1.1 convolution_convert_fusion.1
  12.4 0.1 reshape.163
  12.5 20.4 %all_to_all.10 = bf16[16,4,3584]{2,1,0:T(4,128)(2,1)S(1)} all-to-all(bf16[16,4,3584]{2,1,0:T(4,128)(2,1)S(1)} %reshape.163), channel_id=1, replica_groups=mesh['groups'=1,'wide'=16,'tp'=2,'sub'=1] {'wide'}, dimensions={0} | all-to-all | bytes 917504 | tf_op jit(solution)/shard_map/all_to_all | solution.py:62
  33.0 13.3 %all_gather.9 = bf16[32,4,3584]{2,1,0:T(4,128)(2,1)} all-gather(bf16[16,4,3584]{2,1,0:T(4,128)(2,1)S(1)} %all_to_all.10), channel_id=1, replica_groups=mesh['groups'=1,'wide'=16,'tp'=2,'sub'=1] {'tp','sub'}, dimensions={0}, use_global_device_ids=true | all-gather | bytes 1376256 | tf_op jit(solution)/shard_map/all_gather | solution.py:63
  46.3 1.7 %reshape.164 = bf16[128,3584]{1,0:T(8,128)(2,1)S(1)} reshape(bf16[32,4,3584]{2,1,0:T(4,128)(2,1)} %all_gather.9) | data formatting | bytes 1835008 | tf_op jit(solution)/shard_map/reshape | solution.py:64
  47.9 2.7 %fusion.3 = f32[128,512]{1,0:T(8,128)S(1)} fusion(bf16[128,3584]{1,0:T(8,128)(2,1)S(1)} %reshape.164, bf16[1,3584,512]{2,1,0:T(8,128)(2,1)} %param.14), kind=kOutput, calls=%fused_computation.6 | convolution fusion | flops 469762048 | bytes 4849664 | tf_op jit(solution)/shard_map/dot_general | solution.py:27
  50.6 0.0 copy-start.2
  50.6 5.4 %convolution_convert_fusion = bf16[128,3584]{1,0:T(8,128)(2,1)} fusion(bf16[1,512,3584]{2,1,0:T(8,128)(2,1)} %param.16, bf16[128,3584]{1,0:T(8,128)(2,1)S(1)} %reshape.164, bf16[1,3584,512]{2,1,0:T(8,128)(2,1)} %param.15, f32[128,512]{1,0:T(8,128)S(1)} %fusion.3), kind=kOutput, calls=%fused_computation | convolution fusion | flops 940376064 | bytes 9437184 | tf_op jit(solution)/shard_map/dot_general | solution.py:30
  56.0 0.0 copy-start.1
  56.0 0.0 reduce-scatter.2.cloned.1.call-update
  56.8 0.0 copy-done
  56.8 0.0 copy-done.2
  56.8 1.8 %fusion.9 = f32[128,2048]{1,0:T(8,128)} fusion(bf16[1,2048,512]{2,1,0:T(8,128)(2,1)S(1)} %copy-done, bf16[1,128,512]{2,1,0:T(8,128)(2,1)S(1)} %copy-done.2), kind=kOutput, calls=%fused_computation.13 | convolution fusion | flops 268435456 | bytes 3276800 | tf_op jit(solution)/shard_map/rhc,rlc->rhl/dot_general | solution.py:80
  58.6 16.0 %reduce-scatter.2.cloned.1.call-done = bf16[64,3584]{1,0:T(8,128)(2,1)} async-done(((bf16[128,3584]{1,0:T(8,128)(2,1)}), bf16[64,3584]{1,0:T(8,128)(2,1)}) %reduce-scatter.2.cloned.1.call-update) | async-done | bytes 458768 | tf_op jit(solution)/shard_map/reduce_scatter | solution.py:65
  74.5 1.9 %reshape.165 = bf16[16,4,3584]{2,1,0:T(4,128)(2,1)} reshape(bf16[64,3584]{1,0:T(8,128)(2,1)} %reduce-scatter.2.cloned.1.call-done) | data formatting | bytes 917504 | tf_op jit(solution)/shard_map/reshape | solution.py:73
  76.4 5.6 %all-to-all-start.1 = ((bf16[16,4,3584]{2,1,0:T(4,128)(2,1)}), bf16[16,4,3584]{2,1,0:T(4,128)(2,1)}, u32[]{:S(2)}, u32[]{:S(2)}) async-start(bf16[16,4,3584]{2,1,0:T(4,128)(2,1)} %reshape.165), calls=%async_computation.2 | async-start | bytes 917504 | tf_op jit(solution)/shard_map/all_to_all | solution.py:74
  82.1 0.0 copy-done.1
  82.1 1.7 %fusion.47 = (f32[128]{0:T(128)S(1)}, f32[128,2048]{1,0:T(8,128)S(1)}) fusion(f32[128,2048]{1,0:T(8,128)} %fusion.9, bf16[1,64,2048]{2,1,0:T(8,128)(2,1)S(1)} %copy-done.1, bf16[1,64,128]{2,1,0:T(8,128)(2,1)} %param.18, pred[2048]{0:T(1024)(128)(4,1)S(1)} %add_compare_fusion), kind=kOutput, calls=%fused_computation.55 | convolution fusion | flops 34602880 | bytes 2378240 | tf_op jit(solution)/shard_map/rkh,rkl->rhl/dot_general | solution.py:85
  83.8 4.9 %pmax.7 = f32[128]{0:T(128)S(1)} all-reduce(f32[128]{0:T(128)S(1)} %get-tuple-element.6), channel_id=1, replica_groups=mesh['groups'=1,'wide'=16,'tp'=2,'sub'=1] {'tp'}, use_global_device_ids=true, to_apply=%region_8.9 | all-reduce | flops 128 | bytes 1024 | tf_op jit(solution)/shard_map/pmax | solution.py:89
  88.7 0.3 fusion.25
  89.0 4.9 %psum.7 = bf16[128]{0:T(256)(128)(2,1)S(1)} all-reduce(bf16[128]{0:T(256)(128)(2,1)S(1)} %fusion.25), channel_id=1, replica_groups=mesh['groups'=1,'wide'=16,'tp'=2,'sub'=1] {'tp'}, use_global_device_ids=true, to_apply=%region_11.12 | all-reduce | flops 128 | bytes 512 | tf_op jit(solution)/shard_map/psum | solution.py:104
  94.0 0.5 fusion.17
  94.5 5.6 %all-gather = bf16[256,512]{1,0:T(8,128)(2,1)S(1)} all-gather(bf16[128,512]{1,0:T(8,128)(2,1)S(1)} %fusion.17), channel_id=2, replica_groups=mesh['groups'=1,'wide'=16,'tp'=2,'sub'=1] {'tp'}, dimensions={0}, use_global_device_ids=true | all-gather | bytes 393216 | tf_op jit(solution)/shard_map/all_gather | solution.py:100
  100.2 0.7 fusion.31
  100.9 0.0 all-to-all-done.1
  100.9 1.1 %reshape.166 = bf16[64,3584]{1,0:T(8,128)(2,1)S(1)} reshape(bf16[16,4,3584]{2,1,0:T(4,128)(2,1)} %all-to-all-done.1) | data formatting | bytes 917504 | tf_op jit(solution)/shard_map/reshape | solution.py:75
  102.0 0.9 convolution_convert_fusion.2
  (3 shorter events, 0.1 us)
Async XLA Ops:
  7.2 49.6 %copy-start = (bf16[1,2048,512]{2,1,0:T(8,128)(2,1)S(1)}, bf16[1,2048,512]{2,1,0:T(8,128)(2,1)}, u32[]{:S(2)}) copy-start(bf16[1,2048,512]{2,1,0:T(8,128)(2,1)} %param.19) | copy-start | bytes 6291460
  7.2 67.4 %reduce-scatter.2.cloned.1.call-start = ((), (), s32[]{:S(2)}) async-start(), calls=%async_computation.3 | async-start | bytes 1376256 | tf_op jit(solution)/shard_map/reduce_scatter | solution.py:65
  50.6 6.2 %copy-start.2 = (bf16[1,128,512]{2,1,0:T(8,128)(2,1)S(1)}, bf16[1,128,512]{2,1,0:T(8,128)(2,1)}, u32[]{:S(2)}) copy-start(bf16[1,128,512]{2,1,0:T(8,128)(2,1)} %param.17) | copy-start | bytes 393220
  56.0 26.1 %copy-start.1 = (bf16[1,64,2048]{2,1,0:T(8,128)(2,1)S(1)}, bf16[1,64,2048]{2,1,0:T(8,128)(2,1)}, u32[]{:S(2)}) copy-start(bf16[1,64,2048]{2,1,0:T(8,128)(2,1)} %param.20) | copy-start | bytes 786436
  76.4 24.5 %all-to-all-start.1 = ((bf16[16,4,3584]{2,1,0:T(4,128)(2,1)}), bf16[16,4,3584]{2,1,0:T(4,128)(2,1)}, u32[]{:S(2)}, u32[]{:S(2)}) async-start(bf16[16,4,3584]{2,1,0:T(4,128)(2,1)} %reshape.165), calls=%async_computation.2 | async-start | bytes 917504 | tf_op jit(solution)/shard_map/all_to_all | solution.py:74
Sparse Core Ops, SparseCore 0:
  56.2 18.3 reduce-scatter.1
